TPU v7x, 512 devices: a whole 4x8x8 slice. The times are simulated.
512 devices in a mesh: ctx: 64 (over y, z), tp: 8 (over x, core).
Axes of the slice: x: 4, y: 8, z: 8, core: 2. Of those that a mesh axis runs over, the one named last changes fastest.
Arguments:
- inputs: bfloat16 [8192, 4096], P('ctx', 'tp'), may hold values from -6 to 6
- gate_in: bfloat16 [8192, 4096], P('ctx', 'tp'), may hold values from -6 to 6
- b_proj: bfloat16 [8192, 128], P('ctx'), may hold values from -0.5 to 0.5
- c_proj: bfloat16 [8192, 128], P('ctx'), may hold values from -0.5 to 0.5
- log_decay: float32 [32, 8192], P('tp', 'ctx'), may hold values from -0.75 to 0
- w_out: bfloat16 [4096, 4096], P('tp'), may hold values from -0.09375 to 0.09375
- cotangent: bfloat16 [8192, 4096], P(('ctx', 'tp')), may hold values from -6 to 6
Outputs:
- layer_out: bfloat16 [8192, 4096], P(('ctx', 'tp'))
- grad_inputs: bfloat16 [8192, 4096], P('ctx', 'tp')
- grad_gate: bfloat16 [8192, 4096], P('ctx', 'tp')
- grad_b: float32 [8192, 128], P(('ctx', 'tp'))
- grad_c: float32 [8192, 128], P(('ctx', 'tp'))
- grad_decay: float32 [32, 8192], P('tp', 'ctx')
All inputs are finite; a program needn't handle non-finite values.
Results may differ from a plain program's by a relative error of at most 0.017.
Values may be sent and summed in bfloat16 or wider, within the bound.
No kernel may reach another device: no remote copies, remote signals or barrier semaphores. Data moves between devices by JAX's collectives and lax.ppermute only.
A program may use at most 128 MiB of HBM per device.

v0:
```python
import jax
import jax.numpy as jnp
from jax import lax
from jax.sharding import PartitionSpec as P

BLOCK = 128


def entering(shard, axis, combine, identity, reverse):
    count, place = (lax.axis_size(axis), lax.axis_index(axis))
    everything = jax.tree.map(lambda part: lax.all_gather(part, axis), shard)
    start = jax.tree.map(
        lambda part, zero: jnp.broadcast_to(jnp.asarray(zero, part.dtype), part.shape),
        shard,
        identity,
    )

    def lap(k, before):
        at = count - 1 - k if reverse else k
        reached = at > place if reverse else at < place
        new = combine(before, jax.tree.map(lambda part: part[at], everything))
        return jax.tree.map(lambda a, b: jnp.where(reached, a, b), new, before)

    return lax.fori_loop(0, count, lap, start)


def compose(earlier, later_part):
    return (earlier[0] * later_part[0], later_part[0][:, None, None] * earlier[1] + later_part[1])


def carried(block_decay, block_terms, backward):
    if backward:
        block_decay = jnp.flip(block_decay, 0)
        block_terms = jnp.flip(block_terms, 0)
    head_count = block_decay.shape[1]

    def local_step(running, packed):
        state_level, product = running
        decay_step, term_block = packed
        return (
            (decay_step[:, None, None] * state_level + term_block, decay_step * product),
            (state_level, product),
        )

    initial = (jnp.zeros(block_terms.shape[1:], jnp.float32), jnp.ones((head_count,), jnp.float32))
    (dev_state, dev_decay), (local_in, decay_before) = lax.scan(
        local_step, initial, (block_decay, block_terms)
    )
    identity = (jnp.ones((head_count,), jnp.float32), jnp.zeros(block_terms.shape[1:], jnp.float32))
    if backward:
        incoming = entering((dev_decay, dev_state), "ctx", compose, identity, True)[1]
    else:
        incoming = entering((dev_decay, dev_state), "ctx", compose, identity, False)[1]

    def resume(state_level, packed):
        decay_step, term_block = packed
        return (decay_step[:, None, None] * state_level + term_block, state_level)

    unused, states = lax.scan(resume, incoming, (block_decay, block_terms))
    if backward:
        states = jnp.flip(states, 0)
    return states


def local(inputs, gate_in, b_proj, c_proj, log_decay, w_out, cotangent):
    tok_rows, feature_width = inputs.shape
    head_count = log_decay.shape[0]
    head_dim = feature_width // head_count
    nblocks = tok_rows // BLOCK
    nstate = b_proj.shape[1]
    x_blocks = inputs.reshape(nblocks, BLOCK, head_count, head_dim)
    b_blocks = b_proj.reshape(nblocks, BLOCK, nstate)
    c_blocks = c_proj.reshape(nblocks, BLOCK, nstate)
    d_blocks = jnp.transpose(log_decay.reshape(head_count, nblocks, BLOCK), (1, 2, 0))
    gate_float = gate_in.astype(jnp.float32).reshape(nblocks, BLOCK, head_count, head_dim)
    sigmoid_z = jax.nn.sigmoid(gate_float)
    silu_z = gate_float * sigmoid_z
    position = jnp.arange(BLOCK)
    causal = position[:, None] >= position[None, :]
    lower_ones = causal.astype(jnp.float32)
    cumulative = jnp.einsum("qs,csh->cqh", lower_ones, d_blocks, precision=lax.Precision.HIGHEST)
    final_sum = cumulative[:, -1, :]
    block_decay = jnp.exp(final_sum)
    tail_weight = jnp.exp(final_sum[:, None, :] - cumulative)
    exp_cum = jnp.exp(cumulative)
    column_cum = jnp.transpose(cumulative, (0, 2, 1))
    differ = column_cum[:, :, :, None] - column_cum[:, :, None, :]
    decay_mat = jnp.where(causal, jnp.exp(jnp.minimum(differ, 0.0)), 0.0)
    scores = jnp.einsum("cqn,ckn->cqk", c_blocks, b_blocks, preferred_element_type=jnp.float32)
    mixing_b = (scores[:, None] * decay_mat).astype(jnp.bfloat16)
    y_intra = jnp.einsum("chqk,ckhp->cqhp", mixing_b, x_blocks, preferred_element_type=jnp.float32)
    weighted = (x_blocks.astype(jnp.float32) * tail_weight[..., None]).astype(jnp.bfloat16)
    block_state = jnp.einsum(
        "cqhp,cqn->chpn", weighted, b_blocks, preferred_element_type=jnp.float32
    )
    state_in = carried(block_decay, block_state, False)
    state_b = state_in.astype(jnp.bfloat16)
    y_inter = (
        jnp.einsum("cqn,chpn->cqhp", c_blocks, state_b, preferred_element_type=jnp.float32)
        * exp_cum[..., None]
    )
    y_full = y_intra + y_inter
    gated_out = (y_full * silu_z).astype(jnp.bfloat16).reshape(tok_rows, feature_width)
    layer_out = lax.psum_scatter(
        jnp.dot(gated_out, w_out, preferred_element_type=jnp.float32).astype(jnp.bfloat16),
        "tp",
        scatter_dimension=0,
        tiled=True,
    )
    state_in, state_b, y_inter, y_full, layer_out = (state_in, state_b, y_inter, y_full, layer_out)
    dgated = lax.dot_general(
        lax.all_gather(cotangent, "tp", axis=0, tiled=True),
        w_out,
        (((1,), (1,)), ((), ())),
        preferred_element_type=jnp.float32,
    )
    dgated = dgated.reshape(nblocks, BLOCK, head_count, head_dim)
    grad_y = dgated * silu_z
    grad_w = (grad_y * exp_cum[..., None]).astype(jnp.bfloat16)
    injected = jnp.einsum("cqhp,cqn->chpn", grad_w, c_blocks, preferred_element_type=jnp.float32)
    adjoint_next = carried(block_decay, injected, True)
    dgated, grad_y, grad_w, adjoint_next = (dgated, grad_y, grad_w, adjoint_next)
    grad_gate = (dgated * y_full * (sigmoid_z + gate_float * sigmoid_z * (1.0 - sigmoid_z))).astype(
        jnp.bfloat16
    )
    grad_gate = grad_gate.reshape(tok_rows, feature_width)
    grad_y_b = grad_y.astype(jnp.bfloat16)
    adjoint_b = adjoint_next.astype(jnp.bfloat16)
    pair_dots = jnp.einsum(
        "cqhp,ckhp->chqk", grad_y_b, x_blocks, preferred_element_type=jnp.float32
    )
    dmix = pair_dots * decay_mat
    dmix_b = dmix.astype(jnp.bfloat16)
    state_dx = (
        jnp.einsum("ckn,chpn->ckhp", b_blocks, adjoint_b, preferred_element_type=jnp.float32)
        * tail_weight[..., None]
    )
    grad_inputs = (
        jnp.einsum("chqk,cqhp->ckhp", mixing_b, grad_y_b, preferred_element_type=jnp.float32)
        + state_dx
    )
    grad_inputs = grad_inputs.astype(jnp.bfloat16).reshape(tok_rows, feature_width)
    b_terms = jnp.einsum("chqk,cqn->ckn", dmix_b, c_blocks, preferred_element_type=jnp.float32)
    b_terms = b_terms + jnp.einsum(
        "ckhp,chpn->ckn", weighted, adjoint_b, preferred_element_type=jnp.float32
    )
    c_terms = jnp.einsum("chqk,ckn->cqn", dmix_b, b_blocks, preferred_element_type=jnp.float32)
    c_terms = c_terms + jnp.einsum(
        "cqhp,chpn->cqn", grad_w, state_b, preferred_element_type=jnp.float32
    )
    grad_b, grad_c = (
        lax.psum_scatter(
            b_terms.reshape(tok_rows, nstate).astype(jnp.bfloat16),
            "tp",
            scatter_dimension=0,
            tiled=True,
        ).astype(jnp.float32),
        lax.psum_scatter(
            c_terms.reshape(tok_rows, nstate).astype(jnp.bfloat16),
            "tp",
            scatter_dimension=0,
            tiled=True,
        ).astype(jnp.float32),
    )
    cross_terms = dmix * scores[:, None]
    decay_flow = jnp.transpose(jnp.sum(cross_terms, 3) - jnp.sum(cross_terms, 2), (0, 2, 1))
    outflow = jnp.sum(x_blocks.astype(jnp.float32) * state_dx, 3)
    decay_flow = decay_flow + jnp.sum(grad_y * y_inter, 3) - outflow
    closing = jnp.sum(outflow, 1) + block_decay * jnp.sum(adjoint_next * state_in, (2, 3))
    decay_flow = decay_flow.at[:, -1, :].add(closing)
    grad_decay = jnp.einsum("ut,cuh->cth", lower_ones, decay_flow, precision=lax.Precision.HIGHEST)
    grad_decay = jnp.transpose(grad_decay, (2, 0, 1)).reshape(head_count, tok_rows)
    return (layer_out, grad_inputs, grad_gate, grad_b, grad_c, grad_decay)


def solution(mesh):
    in_specs = (
        P("ctx", "tp"),
        P("ctx", "tp"),
        P("ctx", None),
        P("ctx", None),
        P("tp", "ctx"),
        P("tp", None),
        P(("ctx", "tp"), None),
    )
    out_specs = (
        P(("ctx", "tp"), None),
        P("ctx", "tp"),
        P("ctx", "tp"),
        P(("ctx", "tp"), None),
        P(("ctx", "tp"), None),
        P("tp", "ctx"),
    )
    return jax.shard_map(local, mesh=mesh, in_specs=in_specs, out_specs=out_specs, check_vma=False)
```

profile of v0, /device:TPU:8, one launch (start us, length us, event | category | flops | bytes accessed | tf_op | source)
XLA Modules:
  0.0 479.4 jit_solution(16107612873647827048)
XLA Ops:
  9.3 1.8 convolution_add_fusion.1
  11.4 32.1 %all-gather.7.cloned.1.call-done = bf16[128,4096]{1,0:T(8,128)(2,1)} async-done(((bf16[16,4096]{1,0:T(8,128)(2,1)}), bf16[128,4096]{1,0:T(8,128)(2,1)}) %all-gather.7.cloned.1.call-update) | async-done | bytes 1048592 | tf_op jit(solution)/shard_map/all_gather | solution.py:112
  43.5 4.0 fusion.39
  49.0 45.2 %all-gather = f32[64,1,4]{2,1,0:T(1,128)S(1)} all-gather(f32[1,1,4]{2,1,0:T(1,128)S(1)} %copy.53), channel_id=2, replica_groups=mesh['ctx'=64,'tp'=8] {'ctx'}, dimensions={0}, use_global_device_ids=true | all-gather | bytes 1040 | tf_op jit(solution)/shard_map/all_gather | solution.py:11
  95.1 91.4 %all-gather.9.cloned.1.call-done = f32[256,128,128]{2,1,0:T(8,128)} async-done(((f32[4,128,128]{2,1,0:T(8,128)}), f32[256,128,128]{2,1,0:T(8,128)}) %all-gather.9.cloned.1.call-update) | async-done | bytes 16777232 | tf_op jit(solution)/shard_map/all_gather | solution.py:11
  186.5 70.2 %while.21 = (s32[]{:T(128)}, f32[4,128,128]{2,1,0:T(8,128)S(1)}, s32[]{:T(128)}, f32[64,4]{1,0:T(8,128)S(1)}, f32[64,4,128,128]{3,2,1,0:T(8,128)}, /*index=5*/s32[]{:T(128)}, s32[]{:T(128)}) while((s32[]{:T(128)}, f32[4,128,128]{2,1,0:T(8,128)S(1)}, s32[]{:T(128)}, f32[64,4]{1,0:T(8,128)S(1)}, f32[64,4,128,128]{3,2,1,0:T(8,128)}, ...), condition=%wide.region_1.2_spmd.clone, body=%wide.region_0.1_spmd.clone.sunk | while | flops 262148 | bytes 786585 | solution.py:24
  201.8 1.1 fusion.59
  210.5 1.1 fusion.59
  217.1 1.1 fusion.59
  221.5 1.1 fusion.59
  224.8 1.1 fusion.59
  229.2 1.1 fusion.59
  243.4 1.1 fusion.59
  244.6 1.1 fusion.59
  252.3 1.1 fusion.59
  254.5 1.1 fusion.59
  255.6 1.1 fusion.59
  258.2 69.4 %all-gather.11.cloned.1.call-done = f32[256,128,128]{2,1,0:T(8,128)} async-done(((f32[4,128,128]{2,1,0:T(8,128)}), f32[256,128,128]{2,1,0:T(8,128)}) %all-gather.11.cloned.1.call-update) | async-done | bytes 16777232 | tf_op jit(solution)/shard_map/all_gather | solution.py:11
  327.6 70.8 %while.22 = (s32[]{:T(128)}, f32[4,128,128]{2,1,0:T(8,128)S(1)}, s32[]{:T(128)}, f32[64,4]{1,0:T(8,128)S(1)}, f32[64,4,128,128]{3,2,1,0:T(8,128)}, /*index=5*/s32[]{:T(128)}, s32[]{:T(128)}, s32[]{:T(128)}, s32[]{:T(128)}) while((s32[]{:T(128)}, f32[4,128,128]{2,1,0:T(8,128)S(1)}, s32[]{:T(128)}, f32[64,4]{1,0:T(8,128)S(1)}, ...), condition=%wide.region_4.5_spmd.clone, body=%wide.region_3.4_spmd.clone.sunk | while | flops 262152 | bytes 786647 | solution.py:24
  399.5 3.9 convolution_convert_fusion
  404.3 1.3 convert_element_type.112
  408.2 25.1 %reduce-scatter.6.cloned.1.call-done = bf16[16,128]{1,0:T(8,128)(2,1)} async-done(((bf16[128,128]{1,0:T(8,128)(2,1)}), bf16[16,128]{1,0:T(8,128)(2,1)}) %reduce-scatter.6.cloned.1.call-update) | async-done | bytes 4112 | tf_op jit(solution)/shard_map/reduce_scatter | solution.py:152
  433.3 1.3 convert_element_type.110
  434.5 38.0 %reduce-scatter.4.cloned.1.call-done = bf16[16,4096]{1,0:T(8,128)(2,1)} async-done(((bf16[128,4096]{1,0:T(8,128)(2,1)}), bf16[16,4096]{1,0:T(8,128)(2,1)}) %reduce-scatter.4.cloned.1.call-update) | async-done | bytes 131088 | tf_op jit(solution)/shard_map/reduce_scatter | solution.py:104
  (304 shorter events, 135.1 us)
Async XLA Ops:
  7.2 2.1 copy-start
  7.2 40.3 %copy-start.2 = (bf16[128,512]{1,0:T(8,128)(2,1)S(1)}, bf16[128,512]{1,0:T(8,128)(2,1)}, u32[]{:S(2)}) copy-start(bf16[128,512]{1,0:T(8,128)(2,1)} %param.14) | copy-start | bytes 393220
  7.2 36.3 %all-gather.7.cloned.1.call-start = ((), (), s32[]{:S(2)}) async-start(), calls=%async_computation.4 | async-start | bytes 1179648 | tf_op jit(solution)/shard_map/all_gather | solution.py:112
  7.9 178.5 %all-gather.9.cloned.1.call-start = ((), (), s32[]{:S(2)}) async-start(), calls=%async_computation.7 | async-start | bytes 17039360 | tf_op jit(solution)/shard_map/all_gather | solution.py:11
  9.1 38.5 %copy-start.3 = (bf16[128,128]{1,0:T(8,128)(2,1)S(1)}, bf16[128,128]{1,0:T(8,128)(2,1)}, u32[]{:S(2)}) copy-start(bf16[128,128]{1,0:T(8,128)(2,1)} %param.16) | copy-start | bytes 98308
  11.1 37.5 %copy-start.1 = (bf16[128,512]{1,0:T(8,128)(2,1)S(1)}, bf16[128,512]{1,0:T(8,128)(2,1)}, u32[]{:S(2)}) copy-start(bf16[128,512]{1,0:T(8,128)(2,1)} %param.13) | copy-start | bytes 393220
  11.2 316.5 %all-gather.11.cloned.1.call-start = ((), (), s32[]{:S(2)}) async-start(), calls=%async_computation.8 | async-start | bytes 17039360 | tf_op jit(solution)/shard_map/all_gather | solution.py:11
  48.6 355.7 %reduce-scatter.8.cloned.1.call-start = ((), (), s32[]{:S(2)}) async-start(), calls=%async_computation.6 | async-start | bytes 36864 | tf_op jit(solution)/shard_map/reduce_scatter | solution.py:158
  257.8 175.4 %reduce-scatter.6.cloned.1.call-start = ((), (), s32[]{:S(2)}) async-start(), calls=%async_computation.5 | async-start | bytes 36864 | tf_op jit(solution)/shard_map/reduce_scatter | solution.py:152
  399.5 73.1 %reduce-scatter.4.cloned.1.call-start = ((), (), s32[]{:S(2)}) async-start(), calls=%async_computation.3 | async-start | bytes 1179648 | tf_op jit(solution)/shard_map/reduce_scatter | solution.py:104
Sparse Core Ops, SparseCore 0:
  10.2 33.2 all-gather.6
  46.5 139.9 all-gather.8
  189.5 138.1 all-gather.10
  330.9 33.6 reduce-scatter.7
  399.6 33.5 reduce-scatter.5
  436.5 36.0 reduce-scatter.3
where the time goes:
time: 484 us; the launch traced here: 479 us
  waiting for transfers between devices  257 us (53%)
  other arithmetic  138 us (29%)
  blocking collectives  45.2 us (9%)
  matrix products  15.8 us (3%)
  between operations  14.3 us (3%)
    all_gather x2, waiting for transfers between devices, entering(): everything = jax.tree.map(lambda part: lax.all_gather(part, axis), shard)  161 us
    select_n x128, other arithmetic, lap(): return jax.tree.map(lambda a, b: jnp.where(reached, a, b), new, before)  135 us
    all_gather x1, blocking collectives, entering(): everything = jax.tree.map(lambda part: lax.all_gather(part, axis), shard)  45.2 us
    reduce_scatter x1, waiting for transfers between devices, local(): lax.psum_scatter(jnp.dot(gated_out, w_out, preferred_element_type=jnp.flo...  38 us
    all_gather x1, waiting for transfers between devices, local(): lax.all_gather(cotangent, 'tp', axis=0, tiled=True)  32.1 us
    reduce_scatter x1, waiting for transfers between devices, local(): lax.psum_scatter(b_terms.reshape(tok_rows, nstate).astype(jnp.bfloat16),...  25.1 us
  transfers between devices with their start and end apart: 6, of which 5 were waited for; matrix products, arithmetic and copies ran while one was open for 33% of the time, Pallas kernels for 0%

commit v1 on v0

--- a/solution.py
+++ b/solution.py
@@ -4,6 +4,22 @@
 from jax.sharding import PartitionSpec as P
 
 BLOCK = 128
+
+
+def collect(x, axis, dim):
+    ways, here, lap = (lax.axis_size(axis), lax.axis_index(axis), x.shape[dim])
+    shape = [n * ways if d == dim else n for d, n in enumerate(x.shape)]
+    full = lax.dynamic_update_slice_in_dim(jnp.zeros(shape, x.dtype), x, here * lap, axis=dim)
+    going_up = going_down = x
+    for far in range(1, ways // 2 + 1):
+        going_up = lax.ppermute(going_up, axis, [(d, (d + 1) % ways) for d in range(ways)])
+        full = lax.dynamic_update_slice_in_dim(full, going_up, (here - far) % ways * lap, axis=dim)
+        if 2 * far < ways:
+            going_down = lax.ppermute(going_down, axis, [(d, (d - 1) % ways) for d in range(ways)])
+            full = lax.dynamic_update_slice_in_dim(
+                full, going_down, (here + far) % ways * lap, axis=dim
+            )
+    return full
 
 
 def entering(shard, axis, combine, identity, reverse):
@@ -109,7 +125,7 @@
     )
     state_in, state_b, y_inter, y_full, layer_out = (state_in, state_b, y_inter, y_full, layer_out)
     dgated = lax.dot_general(
-        lax.all_gather(cotangent, "tp", axis=0, tiled=True),
+        collect(cotangent, "tp", 0),
         w_out,
         (((1,), (1,)), ((), ())),
         preferred_element_type=jnp.float32,

time: 484 us -> 453 us (0.936)
  waiting for transfers between devices: 257 us -> 213 us
  starting transfers between devices: 0.24 us -> 9.08 us
    all_gather x1 -> x0, waiting for transfers between devices: 32.1 us -> none  [local(): lax.all_gather(cotangent, 'tp', axis=0, tiled=True)]
    all_gather x2, waiting for transfers between devices: 161 us -> 137 us  [entering(): everything = jax.tree.map(lambda part: lax.all_gather(part, axis), shard)]
    ppermute x0 -> x7, waiting for transfers between devices: none -> 12.2 us  [the longest x4 12.2 us: collect(): lax.ppermute(going_up, axis, [(d, (d + 1) % ways) for d in range(ways)])]
    ppermute x0 -> x7, starting transfers between devices: none -> 8.88 us  [the longest x3 8.85 us: collect(): lax.ppermute(going_down, axis, [(d, (d - 1) % ways) for d in range(ways)])]
  transfers between devices with their start and end apart: 6 -> 12, of which waited for: 5 -> 8; matrix products, arithmetic and copies ran while one was open for 33% -> 35% of each run, Pallas kernels for 0% -> 0%
where the time goes in v1:
time: 453 us; the launch traced here: 448 us
  waiting for transfers between devices  213 us (47%)
  other arithmetic  138 us (30%)
  blocking collectives  48.5 us (11%)
  matrix products  15.5 us (3%)
  between operations  14.2 us (3%)
  starting transfers between devices  9.08 us (2%)
  local copies, waits for them, and re-layouts  5.4 us (1%)
  loops' own time  4.69 us (1%)
    all_gather x2, waiting for transfers between devices, entering(): everything = jax.tree.map(lambda part: lax.all_gather(part, axis), shard)  137 us
    select_n x128, other arithmetic, lap(): return jax.tree.map(lambda a, b: jnp.where(reached, a, b), new, before)  135 us
    all_gather x1, blocking collectives, entering(): everything = jax.tree.map(lambda part: lax.all_gather(part, axis), shard)  48.5 us
    reduce_scatter x1, waiting for transfers between devices, local(): lax.psum_scatter(jnp.dot(gated_out, w_out, preferred_element_type=jnp.flo...  38.1 us
    reduce_scatter x1, waiting for transfers between devices, local(): lax.psum_scatter(b_terms.reshape(tok_rows, nstate).astype(jnp.bfloat16),...  25 us
    ppermute x4, waiting for transfers between devices, collect(): lax.ppermute(going_up, axis, [(d, (d + 1) % ways) for d in range(ways)])  12.2 us
  transfers between devices with their start and end apart: 12, of which 8 were waited for; matrix products, arithmetic and copies ran while one was open for 35% of the time, Pallas kernels for 0%

profile of v1, /device:TPU:8, one launch (start us, length us, event | category | flops | bytes accessed | tf_op | source)
XLA Modules:
  0.0 448.4 jit_solution(6470417479673365859)
XLA Ops:
  8.5 1.8 convolution_add_fusion.1
  10.5 2.9 collective-permute-start.1
  14.8 1.5 collective-permute-done
  16.3 3.0 collective-permute-start.3
  19.3 2.6 collective-permute-done.2
  21.9 3.0 collective-permute-start.5
  24.9 2.6 collective-permute-done.4
  27.5 5.5 %collective-permute-done.6 = bf16[16,4096]{1,0:T(8,128)(2,1)S(1)} collective-permute-done((bf16[16,4096]{1,0:T(8,128)(2,1)S(1)}, bf16[16,4096]{1,0:T(8,128)(2,1)S(1)}, u32[]{:S(2)}, u32[]{:S(2)}) %collective-permute-start.6) | collective-permute-done | bytes 131104 | tf_op jit(solution)/shard_map/ppermute | solution.py:15
  33.1 3.7 fusion.39
  38.3 48.5 %all-gather = f32[64,1,4]{2,1,0:T(1,128)S(1)} all-gather(f32[1,1,4]{2,1,0:T(1,128)S(1)} %copy.53), channel_id=2, replica_groups=mesh['ctx'=64,'tp'=8] {'ctx'}, dimensions={0}, use_global_device_ids=true | all-gather | bytes 1040 | tf_op jit(solution)/shard_map/all_gather | solution.py:27
  87.7 68.2 %all-gather.6.cloned.1.call-done = f32[256,128,128]{2,1,0:T(8,128)} async-done(((f32[4,128,128]{2,1,0:T(8,128)}), f32[256,128,128]{2,1,0:T(8,128)}) %all-gather.6.cloned.1.call-update) | async-done | bytes 16777232 | tf_op jit(solution)/shard_map/all_gather | solution.py:27
  155.9 70.1 %while.21 = (s32[]{:T(128)}, f32[4,128,128]{2,1,0:T(8,128)S(1)}, s32[]{:T(128)}, f32[64,4]{1,0:T(8,128)S(1)}, f32[64,4,128,128]{3,2,1,0:T(8,128)}, /*index=5*/s32[]{:T(128)}, s32[]{:T(128)}) while((s32[]{:T(128)}, f32[4,128,128]{2,1,0:T(8,128)S(1)}, s32[]{:T(128)}, f32[64,4]{1,0:T(8,128)S(1)}, f32[64,4,128,128]{3,2,1,0:T(8,128)}, ...), condition=%wide.region_1.2_spmd.clone, body=%wide.region_0.1_spmd.clone.sunk | while | flops 262148 | bytes 786585 | solution.py:40
  186.6 1.1 fusion.59
  212.9 1.1 fusion.59
  221.7 1.1 fusion.59
  223.9 1.1 fusion.59
  225.0 1.1 fusion.59
  227.7 69.1 %all-gather.8.cloned.1.call-done = f32[256,128,128]{2,1,0:T(8,128)} async-done(((f32[4,128,128]{2,1,0:T(8,128)}), f32[256,128,128]{2,1,0:T(8,128)}) %all-gather.8.cloned.1.call-update) | async-done | bytes 16777232 | tf_op jit(solution)/shard_map/all_gather | solution.py:27
  296.9 70.9 %while.22 = (s32[]{:T(128)}, f32[4,128,128]{2,1,0:T(8,128)S(1)}, s32[]{:T(128)}, f32[64,4]{1,0:T(8,128)S(1)}, f32[64,4,128,128]{3,2,1,0:T(8,128)}, /*index=5*/s32[]{:T(128)}, s32[]{:T(128)}, s32[]{:T(128)}, s32[]{:T(128)}) while((s32[]{:T(128)}, f32[4,128,128]{2,1,0:T(8,128)S(1)}, s32[]{:T(128)}, f32[64,4]{1,0:T(8,128)S(1)}, ...), condition=%wide.region_4.5_spmd.clone, body=%wide.region_3.4_spmd.clone.sunk | while | flops 262152 | bytes 786647 | solution.py:40
  368.8 3.9 convolution_convert_fusion
  373.5 1.3 convert_element_type.112
  377.4 25.0 %reduce-scatter.6.cloned.1.call-done = bf16[16,128]{1,0:T(8,128)(2,1)} async-done(((bf16[128,128]{1,0:T(8,128)(2,1)}), bf16[16,128]{1,0:T(8,128)(2,1)}) %reduce-scatter.6.cloned.1.call-update) | async-done | bytes 4112 | tf_op jit(solution)/shard_map/reduce_scatter | solution.py:168
  402.5 1.3 convert_element_type.110
  403.7 38.1 %reduce-scatter.4.cloned.1.call-done = bf16[16,4096]{1,0:T(8,128)(2,1)} async-done(((bf16[128,4096]{1,0:T(8,128)(2,1)}), bf16[16,4096]{1,0:T(8,128)(2,1)}) %reduce-scatter.4.cloned.1.call-update) | async-done | bytes 131088 | tf_op jit(solution)/shard_map/reduce_scatter | solution.py:120
  (325 shorter events, 142.0 us)
Async XLA Ops:
  7.2 1.4 copy-start
  7.2 148.7 %all-gather.6.cloned.1.call-start = ((), (), s32[]{:S(2)}) async-start(), calls=%async_computation.6 | async-start | bytes 17039360 | tf_op jit(solution)/shard_map/all_gather | solution.py:27
  10.4 286.5 %all-gather.8.cloned.1.call-start = ((), (), s32[]{:S(2)}) async-start(), calls=%async_computation.7 | async-start | bytes 17039360 | tf_op jit(solution)/shard_map/all_gather | solution.py:27
  10.4 5.8 %collective-permute-start = (bf16[16,4096]{1,0:T(8,128)(2,1)}, bf16[16,4096]{1,0:T(8,128)(2,1)S(1)}, u32[]{:S(2)}, u32[]{:S(2)}) collective-permute-start(bf16[16,4096]{1,0:T(8,128)(2,1)} %param.19), channel_id=1, source_target_pairs={{0,1},{1,2},{2,3},{3,4},{4,5},{5,6},{6,7},{7,0},{8,9},{9,10},{10,1... | collective-permute-start | bytes 393224 | tf_op jit(solution)/shard_map/ppermute | solution.py:15
  10.5 5.8 %collective-permute-start.1 = (bf16[16,4096]{1,0:T(8,128)(2,1)}, bf16[16,4096]{1,0:T(8,128)(2,1)S(1)}, u32[]{:S(2)}, u32[]{:S(2)}) collective-permute-start(bf16[16,4096]{1,0:T(8,128)(2,1)} %param.19), channel_id=1, source_target_pairs={{0,7},{1,0},{2,1},{3,2},{4,3},{5,4},{6,5},{7,6},{8,15},{9,8},{10,9... | collective-permute-start | bytes 393224 | tf_op jit(solution)/shard_map/ppermute | solution.py:18
  14.4 22.4 %copy-start.2 = (bf16[128,512]{1,0:T(8,128)(2,1)S(1)}, bf16[128,512]{1,0:T(8,128)(2,1)}, u32[]{:S(2)}) copy-start(bf16[128,512]{1,0:T(8,128)(2,1)} %param.14) | copy-start | bytes 393220
  14.7 22.2 %copy-start.3 = (bf16[128,128]{1,0:T(8,128)(2,1)S(1)}, bf16[128,128]{1,0:T(8,128)(2,1)}, u32[]{:S(2)}) copy-start(bf16[128,128]{1,0:T(8,128)(2,1)} %param.16) | copy-start | bytes 98308
  16.3 5.6 %collective-permute-start.2 = (bf16[16,4096]{1,0:T(8,128)(2,1)S(1)}, bf16[16,4096]{1,0:T(8,128)(2,1)S(1)}, u32[]{:S(2)}, u32[]{:S(2)}) collective-permute-start(bf16[16,4096]{1,0:T(8,128)(2,1)S(1)} %collective-permute-done), channel_id=1, source_target_pairs={{0,1},{1,2},{2,3},{3,4},{4,5},{5,6},{6,7},{7,0},{8,9},{9,10},{10,1... | collective-permute-start | bytes 393224 | tf_op jit(solution)/shard_map/ppermute | solution.py:15
  16.3 5.6 %collective-permute-start.3 = (bf16[16,4096]{1,0:T(8,128)(2,1)S(1)}, bf16[16,4096]{1,0:T(8,128)(2,1)S(1)}, u32[]{:S(2)}, u32[]{:S(2)}) collective-permute-start(bf16[16,4096]{1,0:T(8,128)(2,1)S(1)} %collective-permute-done.1), channel_id=1, source_target_pairs={{0,7},{1,0},{2,1},{3,2},{4,3},{5,4},{6,5},{7,6},{8,15},{9,8},{10,9... | collective-permute-start | bytes 393224 | tf_op jit(solution)/shard_map/ppermute | solution.py:18
  21.9 5.6 %collective-permute-start.4 = (bf16[16,4096]{1,0:T(8,128)(2,1)S(1)}, bf16[16,4096]{1,0:T(8,128)(2,1)S(1)}, u32[]{:S(2)}, u32[]{:S(2)}) collective-permute-start(bf16[16,4096]{1,0:T(8,128)(2,1)S(1)} %collective-permute-done.2), channel_id=1, source_target_pairs={{0,1},{1,2},{2,3},{3,4},{4,5},{5,6},{6,7},{7,0},{8,9},{9,10},{10,1... | collective-permute-start | bytes 393224 | tf_op jit(solution)/shard_map/ppermute | solution.py:15
  21.9 5.6 %collective-permute-start.5 = (bf16[16,4096]{1,0:T(8,128)(2,1)S(1)}, bf16[16,4096]{1,0:T(8,128)(2,1)S(1)}, u32[]{:S(2)}, u32[]{:S(2)}) collective-permute-start(bf16[16,4096]{1,0:T(8,128)(2,1)S(1)} %collective-permute-done.3), channel_id=1, source_target_pairs={{0,7},{1,0},{2,1},{3,2},{4,3},{5,4},{6,5},{7,6},{8,15},{9,8},{10,9... | collective-permute-start | bytes 393224 | tf_op jit(solution)/shard_map/ppermute | solution.py:18
  24.9 13.2 %copy-start.1 = (bf16[128,512]{1,0:T(8,128)(2,1)S(1)}, bf16[128,512]{1,0:T(8,128)(2,1)}, u32[]{:S(2)}) copy-start(bf16[128,512]{1,0:T(8,128)(2,1)} %param.13) | copy-start | bytes 393220
  27.5 5.6 %collective-permute-start.6 = (bf16[16,4096]{1,0:T(8,128)(2,1)S(1)}, bf16[16,4096]{1,0:T(8,128)(2,1)S(1)}, u32[]{:S(2)}, u32[]{:S(2)}) collective-permute-start(bf16[16,4096]{1,0:T(8,128)(2,1)S(1)} %collective-permute-done.4), channel_id=1, source_target_pairs={{0,1},{1,2},{2,3},{3,4},{4,5},{5,6},{6,7},{7,0},{8,9},{9,10},{10,1... | collective-permute-start | bytes 393224 | tf_op jit(solution)/shard_map/ppermute | solution.py:15
  37.9 335.6 %reduce-scatter.8.cloned.1.call-start = ((), (), s32[]{:S(2)}) async-start(), calls=%async_computation.5 | async-start | bytes 36864 | tf_op jit(solution)/shard_map/reduce_scatter | solution.py:174
  227.5 174.9 %reduce-scatter.6.cloned.1.call-start = ((), (), s32[]{:S(2)}) async-start(), calls=%async_computation.4 | async-start | bytes 36864 | tf_op jit(solution)/shard_map/reduce_scatter | solution.py:168
  368.8 73.1 %reduce-scatter.4.cloned.1.call-start = ((), (), s32[]{:S(2)}) async-start(), calls=%async_computation.3 | async-start | bytes 1179648 | tf_op jit(solution)/shard_map/reduce_scatter | solution.py:120
Sparse Core Ops, SparseCore 0:
  11.0 144.8 all-gather.5
  158.9 137.8 all-gather.7
  300.2 33.6 reduce-scatter.7
  368.9 33.5 reduce-scatter.5
  405.7 36.0 reduce-scatter.3
